TPU v7x, 32 devices: a whole 2x2x4 slice. The times are simulated.
32 devices in a mesh: fsdp: 4 (over y, core), tensor: 8 (over z, x).
Axes of the slice: x: 2, y: 2, z: 4, core: 2. Of those that a mesh axis runs over, the one named last changes fastest.
Arguments:
- activations: bfloat16 [4096, 8192], P('fsdp', 'tensor'), may hold values from -6 to 6
- first_factor: bfloat16 [64, 128, 512], P('tensor', 'fsdp'), may hold values from -0.5 to 0.5
- second_factor: bfloat16 [64, 512, 512], P('tensor', 'fsdp'), may hold values from -0.25 to 0.25
- third_factor: bfloat16 [64, 512, 512], P('tensor', 'fsdp'), may hold values from -0.25 to 0.25
- fourth_factor: bfloat16 [64, 512, 128], P('tensor', 'fsdp'), may hold values from -0.25 to 0.25
- out_grad: bfloat16 [4096, 8192], P('fsdp', 'tensor'), may hold values from -6 to 6
Outputs:
- result: bfloat16 [4096, 8192], P('fsdp', 'tensor')
- in_grad: bfloat16 [4096, 8192], P('fsdp', 'tensor')
- first_grad: float32 [64, 128, 512], P('tensor', 'fsdp')
- second_grad: float32 [64, 512, 512], P('tensor', 'fsdp')
- third_grad: float32 [64, 512, 512], P('tensor', 'fsdp')
- fourth_grad: float32 [64, 512, 128], P('tensor', 'fsdp')
All inputs are finite; a program needn't handle non-finite values.
Results may differ from a plain program's by a relative error of at most 0.014.
Values may be sent and summed in bfloat16 or wider, within the bound.
A program may use at most 128 MiB of HBM per device.

v0:
```python
import jax
import jax.numpy as jnp
from jax import lax
from jax.sharding import PartitionSpec as P

D = 8192
NB = 64
HB = 512


def gelu_value(v):
    return 0.5 * v * (1.0 + lax.erf(v * 0.7071067811865476))


def gelu_slope(v):
    return (
        0.5 * (1.0 + lax.erf(v * 0.7071067811865476))
        + v * jnp.exp(-0.5 * v * v) * 0.3989422804014327
    )


def fetch_first(shard):
    return lax.all_gather(shard, "fsdp", axis=1, tiled=True)


def fetch_second(shard):
    return lax.all_gather(shard, "fsdp", axis=1, tiled=True)


def fetch_third(shard):
    return lax.all_gather(shard, "fsdp", axis=1, tiled=True)


def fetch_fourth(shard):
    return lax.all_gather(shard, "fsdp", axis=1, tiled=True)


def split_units(arr):
    return arr.reshape(arr.shape[0], NB, HB // NB, arr.shape[2])


def join_units(received):
    local_blocks = received.shape[1]
    return received.transpose(1, 0, 2, 3).reshape(local_blocks, HB, received.shape[3])


def local(activations, first_factor, second_factor, third_factor, fourth_factor, out_grad):
    f32 = jnp.float32
    bf16 = jnp.bfloat16
    tok = activations.shape[0]
    local_blocks = second_factor.shape[0]
    block_in = D // NB
    inputs = activations.reshape(tok, local_blocks, block_in)
    factors = (
        fetch_first(first_factor),
        fetch_second(second_factor),
        fetch_third(third_factor),
        fetch_fourth(fourth_factor),
    )
    wone, wtwo, wthree, wfour = factors
    first_out = jnp.einsum("tbi,bij->bjt", inputs, wone, preferred_element_type=f32).astype(bf16)
    mixed_part = join_units(
        lax.all_to_all(split_units(first_out), "tensor", split_axis=1, concat_axis=0, tiled=True)
    )
    pre_part = jnp.einsum("cpt,cpm->cmt", mixed_part, wtwo, preferred_element_type=f32)
    hidden_part = gelu_value(pre_part).astype(bf16)
    down_part = jnp.einsum("cmt,cmn->cnt", hidden_part, wthree, preferred_element_type=f32).astype(
        bf16
    )
    back = lax.all_to_all(split_units(down_part), "tensor", split_axis=1, concat_axis=0, tiled=True)
    regrouped = join_units(back)
    result = jnp.einsum("bpt,bpo->tbo", regrouped, wfour, preferred_element_type=f32).astype(bf16)
    result = result.reshape(tok, local_blocks * block_in)
    vone, vtwo, vthree, vfour = (
        fetch_first(first_factor),
        fetch_second(second_factor),
        fetch_third(third_factor),
        fetch_fourth(fourth_factor),
    )
    grad_out = out_grad.reshape(tok, local_blocks, block_in)
    fourth_grad = jnp.einsum("bpt,tbo->bpo", regrouped, grad_out, preferred_element_type=f32)
    dw = jnp.einsum("tbo,bpo->bpt", grad_out, vfour, preferred_element_type=f32).astype(bf16)
    ddown = join_units(
        lax.all_to_all(split_units(dw), "tensor", split_axis=1, concat_axis=0, tiled=True)
    )
    again_out = jnp.einsum("tbi,bij->bjt", inputs, vone, preferred_element_type=f32).astype(bf16)
    mixed_in = join_units(
        lax.all_to_all(split_units(again_out), "tensor", split_axis=1, concat_axis=0, tiled=True)
    )
    pre = jnp.einsum("cpt,cpm->cmt", mixed_in, vtwo, preferred_element_type=f32)
    hidden = gelu_value(pre).astype(bf16)
    third_grad = jnp.einsum("cmt,cnt->cmn", hidden, ddown, preferred_element_type=f32)
    dhidden = jnp.einsum("cnt,cmn->cmt", ddown, vthree, preferred_element_type=f32)
    dpre = (dhidden * gelu_slope(pre)).astype(bf16)
    second_grad = jnp.einsum("cpt,cmt->cpm", mixed_in, dpre, preferred_element_type=f32)
    dz = jnp.einsum("cmt,cpm->cpt", dpre, vtwo, preferred_element_type=f32).astype(bf16)
    dy = join_units(
        lax.all_to_all(split_units(dz), "tensor", split_axis=1, concat_axis=0, tiled=True)
    )
    first_grad = jnp.einsum("tbi,bjt->bij", inputs, dy, preferred_element_type=f32)
    in_grad = jnp.einsum("bjt,bij->tbi", dy, vone, preferred_element_type=f32).astype(bf16)
    in_grad = in_grad.reshape(tok, local_blocks * block_in)
    shares = (
        lax.psum_scatter(
            first_grad.astype(jnp.bfloat16), "fsdp", scatter_dimension=1, tiled=True
        ).astype(jnp.float32),
        lax.psum_scatter(
            second_grad.astype(jnp.bfloat16), "fsdp", scatter_dimension=1, tiled=True
        ).astype(jnp.float32),
        lax.psum_scatter(
            third_grad.astype(jnp.bfloat16), "fsdp", scatter_dimension=1, tiled=True
        ).astype(jnp.float32),
        lax.psum_scatter(
            fourth_grad.astype(jnp.bfloat16), "fsdp", scatter_dimension=1, tiled=True
        ).astype(jnp.float32),
    )
    return (result, in_grad, shares[0], shares[1], shares[2], shares[3])


def solution(mesh):
    in_specs = (
        P("fsdp", "tensor"),
        P("tensor", "fsdp", None),
        P("tensor", "fsdp", None),
        P("tensor", "fsdp", None),
        P("tensor", "fsdp", None),
        P("fsdp", "tensor"),
    )
    out_specs = (
        P("fsdp", "tensor"),
        P("fsdp", "tensor"),
        P("tensor", "fsdp", None),
        P("tensor", "fsdp", None),
        P("tensor", "fsdp", None),
        P("tensor", "fsdp", None),
    )
    return jax.shard_map(local, mesh=mesh, in_specs=in_specs, out_specs=out_specs, check_vma=False)
```

profile of v0, /device:TPU:0, one launch (start us, length us, event | category | flops | bytes accessed | tf_op | source)
XLA Modules:
  0.0 903.7 jit_solution(2316316129718884985)
XLA Ops:
  9.2 20.5 %all-gather.11.cloned.1.call-done = bf16[8,512,128]{1,2,0:T(8,128)(2,1)} async-done(((bf16[8,128,128]{1,2,0:T(8,128)(2,1)}), bf16[8,512,128]{1,2,0:T(8,128)(2,1)}) %all-gather.11.cloned.1.call-update) | async-done | bytes 1048592 | tf_op jit(solution)/shard_map/all_gather | solution.py:35
  29.7 7.6 convert_bitcast_fusion.1
  37.3 8.1 copy.65
  45.4 5.5 all-to-all-start.2
  51.7 18.9 %all-gather.5.cloned.1.call-done = bf16[8,128,512]{2,1,0:T(8,128)(2,1)} async-done(((bf16[8,32,512]{2,1,0:T(8,128)(2,1)}), bf16[8,128,512]{2,1,0:T(8,128)(2,1)}) %all-gather.5.cloned.1.call-update) | async-done | bytes 1048592 | tf_op jit(solution)/shard_map/all_gather | solution.py:23
  70.5 6.8 convert_bitcast_fusion.3
  77.4 8.0 copy.55
  85.4 149.0 %all-to-all-done.2 = bf16[8,64,8,1024]{3,2,0,1:T(8,128)(2,1)} async-done(((bf16[8,64,8,1024]{3,2,0,1:T(8,128)(2,1)}), bf16[8,64,8,1024]{3,2,0,1:T(8,128)(2,1)}, u32[]{:S(2)}, u32[]{:S(2)}) %all-to-all-start.2) | async-done | bytes 8388640 | tf_op jit(solution)/shard_map/all_to_all | solution.py:84
  234.5 5.0 all-to-all-start
  242.1 9.0 %copy.66 = bf16[8,8,8,8,1024]{4,3,0,1,2:T(8,128)(2,1)} copy(bf16[8,8,8,8,1024]{4,3,0,2,1:T(8,128)(2,1)} %bitcast.17) | data formatting | bytes 16777216 | tf_op jit(solution)/shard_map/all_to_all | solution.py:84
  251.1 171.0 %all-to-all-done = bf16[8,64,8,1024]{3,2,0,1:T(8,128)(2,1)} async-done(((bf16[8,64,8,1024]{3,2,0,1:T(8,128)(2,1)}), bf16[8,64,8,1024]{3,2,0,1:T(8,128)(2,1)}, u32[]{:S(2)}, u32[]{:S(2)}) %all-to-all-start) | async-done | bytes 8388640 | tf_op jit(solution)/shard_map/all_to_all | solution.py:63
  422.1 8.5 copy.56
  430.6 14.5 %fusion.7 = (bf16[8,512,1024]{1,2,0:T(8,128)(2,1)}, f32[8,1024,512]{2,1,0:T(8,128)}) fusion(bf16[8,512,1024]{2,1,0:T(8,128)(2,1)} %bitcast.126, bf16[8,512,512]{2,1,0:T(8,128)(2,1)} %all-gather.7.cloned.1.call-done), kind=kOutput, calls=%fused_computation.10 | convolution fusion | flops 4315938816 | bytes 37748736 | tf_op jit(solution)/shard_map/cpt,cpm->cmt/dot_general | solution.py:65
  445.1 14.2 %fusion.5 = bf16[8,512,1024]{1,2,0:T(8,128)(2,1)S(1)} fusion(f32[8,1024,512]{2,1,0:T(8,128)} %get-tuple-element.25, bf16[8,512,1024]{2,1,0:T(8,128)(2,1)} %bitcast.128, bf16[8,512,512]{1,2,0:T(8,128)(2,1)} %all-gather.9.cloned.1.call-done), kind=kOutput, calls=%fused_computation.6 | convolution fusion | flops 4336910336 | bytes 37748736 | tf_op jit(solution)/shard_map/cnt,cmn->cmt/dot_general | solution.py:93
  462.6 6.7 convert_bitcast_fusion
  469.3 8.0 copy.70
  477.3 5.0 all-to-all-start.3
  482.6 11.0 %convolution_convert_fusion = bf16[8,512,512]{2,1,0:T(8,128)(2,1)} fusion(bf16[8,512,1024]{1,2,0:T(8,128)(2,1)} %get-tuple-element.24, bf16[8,512,1024]{2,1,0:T(8,128)(2,1)} %bitcast.129), kind=kOutput, calls=%fused_computation.17 | convolution fusion | flops 4297064448 | bytes 20971520 | tf_op jit(solution)/shard_map/cmt,cnt->cmn/dot_general | solution.py:92
  493.7 10.4 %convert_bitcast_fusion.2 = bf16[8,64,8,1024]{3,2,1,0:T(8,128)(2,1)} fusion(bf16[8,512,1024]{1,2,0:T(8,128)(2,1)} %get-tuple-element.24, bf16[8,512,512]{1,2,0:T(8,128)(2,1)} %all-gather.9.cloned.1.call-done), kind=kOutput, calls=%fused_computation.15 | convolution fusion | flops 4299161600 | bytes 20971520 | tf_op jit(solution)/shard_map/cmt,cmn->cnt/dot_general | solution.py:67
  504.1 8.3 copy.60
  512.3 152.0 %all-to-all-done.3 = bf16[8,64,8,1024]{3,2,0,1:T(8,128)(2,1)} async-done(((bf16[8,64,8,1024]{3,2,0,1:T(8,128)(2,1)}), bf16[8,64,8,1024]{3,2,0,1:T(8,128)(2,1)}, u32[]{:S(2)}, u32[]{:S(2)}) %all-to-all-start.3) | async-done | bytes 8388640 | tf_op jit(solution)/shard_map/all_to_all | solution.py:98
  664.3 5.0 all-to-all-start.1
  669.3 12.2 %convolution_convert_fusion.1 = bf16[8,512,512]{2,1,0:T(8,128)(2,1)} fusion(bf16[8,512,1024]{2,1,0:T(8,128)(2,1)} %bitcast.127, bf16[8,512,1024]{1,2,0:T(8,128)(2,1)} %copy-done.5), kind=kOutput, calls=%fused_computation.18 | convolution fusion | flops 4297064448 | bytes 20971520 | tf_op jit(solution)/shard_map/cpt,cmt->cpm/dot_general | solution.py:95
  681.8 9.1 %copy.71 = bf16[8,8,8,8,1024]{4,3,1,0,2:T(8,128)(2,1)} copy(bf16[8,8,8,8,1024]{4,3,1,2,0:T(8,128)(2,1)} %bitcast.26) | data formatting | bytes 16777216 | tf_op jit(solution)/shard_map/all_to_all | solution.py:98
  691.0 6.1 fusion.26
  698.9 152.5 %all-to-all-done.1 = bf16[8,64,8,1024]{3,2,0,1:T(8,128)(2,1)} async-done(((bf16[8,64,8,1024]{3,2,0,1:T(8,128)(2,1)}), bf16[8,64,8,1024]{3,2,0,1:T(8,128)(2,1)}, u32[]{:S(2)}, u32[]{:S(2)}) %all-to-all-start.1) | async-done | bytes 8388640 | tf_op jit(solution)/shard_map/all_to_all | solution.py:70
  851.5 8.5 copy.61
  860.0 6.8 fusion.23
  872.6 6.5 convolution_convert_fusion.2
  879.1 4.0 copy.78
  883.1 6.0 convolution_convert_fusion.3
  889.1 3.9 copy.77
  (41 shorter events, 20.3 us)
Async XLA Ops:
  7.2 63.4 %copy-start = (bf16[1024,1024]{1,0:T(8,128)(2,1)S(1)}, bf16[1024,1024]{1,0:T(8,128)(2,1)}, u32[]{:S(2)}) copy-start(bf16[1024,1024]{1,0:T(8,128)(2,1)} %param.6) | copy-start | bytes 6291460
  7.2 22.5 %all-gather.11.cloned.1.call-start = ((), (), s32[]{:S(2)}) async-start(), calls=%async_computation.11 | async-start | bytes 1310720 | tf_op jit(solution)/shard_map/all_gather | solution.py:35
  45.4 189.1 %all-to-all-start.2 = ((bf16[8,64,8,1024]{3,2,0,1:T(8,128)(2,1)}), bf16[8,64,8,1024]{3,2,0,1:T(8,128)(2,1)}, u32[]{:S(2)}, u32[]{:S(2)}) async-start(bf16[8,64,8,1024]{3,2,0,1:T(8,128)(2,1)} %copy.65), calls=%async_computation.2 | async-start | bytes 16777216 | tf_op jit(solution)/shard_map/all_to_all | solution.py:84
  50.9 19.6 %all-gather.5.cloned.1.call-start = ((), (), s32[]{:S(2)}) async-start(), calls=%async_computation.8 | async-start | bytes 1310720 | tf_op jit(solution)/shard_map/all_gather | solution.py:23
  85.4 155.3 %copy-start.3 = (bf16[8,128,512]{2,1,0:T(8,128)(2,1)S(1)}, bf16[8,128,512]{2,1,0:T(8,128)(2,1)}, u32[]{:S(2)}) copy-start(bf16[8,128,512]{2,1,0:T(8,128)(2,1)} %param.9) | copy-start | bytes 3145732
  234.5 187.6 %all-to-all-start = ((bf16[8,64,8,1024]{3,2,0,1:T(8,128)(2,1)}), bf16[8,64,8,1024]{3,2,0,1:T(8,128)(2,1)}, u32[]{:S(2)}, u32[]{:S(2)}) async-start(bf16[8,64,8,1024]{3,2,0,1:T(8,128)(2,1)} %copy.55), calls=%async_computation | async-start | bytes 16777216 | tf_op jit(solution)/shard_map/all_to_all | solution.py:63
  239.5 191.1 %all-gather.7.cloned.1.call-start = ((), (), s32[]{:S(2)}) async-start(), calls=%async_computation.9 | async-start | bytes 5242880 | tf_op jit(solution)/shard_map/all_gather | solution.py:27
  240.2 204.9 %all-gather.9.cloned.1.call-start = ((), (), s32[]{:S(2)}) async-start(), calls=%async_computation.10 | async-start | bytes 5242880 | tf_op jit(solution)/shard_map/all_gather | solution.py:31
  445.1 17.5 %copy-start.4 = (bf16[8,512,512]{2,1,0:T(8,128)(2,1)S(1)}, bf16[8,512,512]{2,1,0:T(8,128)(2,1)}, u32[]{:S(2)}) copy-start(bf16[8,512,512]{2,1,0:T(8,128)(2,1)} %all-gather.7.cloned.1.call-done) | copy-start | bytes 12582916
  459.3 3.3 copy-start.5
  477.3 187.0 %all-to-all-start.3 = ((bf16[8,64,8,1024]{3,2,0,1:T(8,128)(2,1)}), bf16[8,64,8,1024]{3,2,0,1:T(8,128)(2,1)}, u32[]{:S(2)}, u32[]{:S(2)}) async-start(bf16[8,64,8,1024]{3,2,0,1:T(8,128)(2,1)} %copy.70), calls=%async_computation.3 | async-start | bytes 16777216 | tf_op jit(solution)/shard_map/all_to_all | solution.py:98
  482.4 384.4 %reduce-scatter.9.cloned.1.call-start = ((), (), s32[]{:S(2)}) async-start(), calls=%async_computation.14 | async-start | bytes 5242880 | tf_op jit(solution)/shard_map/reduce_scatter | solution.py:110
  664.3 187.2 %all-to-all-start.1 = ((bf16[8,64,8,1024]{3,2,0,1:T(8,128)(2,1)}), bf16[8,64,8,1024]{3,2,0,1:T(8,128)(2,1)}, u32[]{:S(2)}, u32[]{:S(2)}) async-start(bf16[8,64,8,1024]{3,2,0,1:T(8,128)(2,1)} %copy.60), calls=%async_computation.1 | async-start | bytes 16777216 | tf_op jit(solution)/shard_map/all_to_all | solution.py:70
  669.3 200.4 %reduce-scatter.7.cloned.1.call-start = ((), (), s32[]{:S(2)}) async-start(), calls=%async_computation.13 | async-start | bytes 5242880 | tf_op jit(solution)/shard_map/reduce_scatter | solution.py:107
  681.6 211.4 %reduce-scatter.5.cloned.1.call-start = ((), (), s32[]{:S(2)}) async-start(), calls=%async_computation.12 | async-start | bytes 1310720 | tf_op jit(solution)/shard_map/reduce_scatter | solution.py:104
  698.9 196.0 %reduce-scatter.11.cloned.1.call-start = ((), (), s32[]{:S(2)}) async-start(), calls=%async_computation.15 | async-start | bytes 1310720 | tf_op jit(solution)/shard_map/reduce_scatter | solution.py:113
  851.5 8.6 copy-start.2
  872.6 10.4 %copy-start.1 = (bf16[8,512,128]{1,2,0:T(8,128)(2,1)S(1)}, bf16[8,512,128]{1,2,0:T(8,128)(2,1)}, u32[]{:S(2)}) copy-start(bf16[8,512,128]{1,2,0:T(8,128)(2,1)} %all-gather.11.cloned.1.call-done) | copy-start | bytes 3145732
Sparse Core Ops, SparseCore 0:
  10.1 19.5 all-gather.10
  53.3 17.1 all-gather.4
  241.9 34.8 all-gather.6
  278.7 35.0 all-gather.8
  493.8 44.8 reduce-scatter.8
  681.7 44.8 reduce-scatter.6
  729.1 24.8 reduce-scatter.4
  866.9 23.1 reduce-scatter.10
where the time goes:
time: 911 us; the launch traced here: 904 us
  waiting for transfers between devices  666 us (73%)
  matrix products  109 us (12%)
  local copies, waits for them, and re-layouts  85.6 us (9%)
  starting transfers between devices  21.7 us (2%)
  between operations  14.5 us (2%)
    all_to_all x1, waiting for transfers between devices, local(): lax.all_to_all(split_units(first_out), 'tensor', split_axis=1, concat_axi...  171 us
    all_to_all x1, waiting for transfers between devices, local(): lax.all_to_all(split_units(down_part), 'tensor', split_axis=1, concat_axi...  153 us
    all_to_all x1, waiting for transfers between devices, local(): lax.all_to_all(split_units(dz), 'tensor', split_axis=1, concat_axis=0, ti...  152 us
    all_to_all x1, waiting for transfers between devices, local(): lax.all_to_all(split_units(dw), 'tensor', split_axis=1, concat_axis=0, ti...  149 us
    reshape x4, local copies, waits for them, and re-layouts, split_units(): return arr.reshape(arr.shape[0], NB, HB // NB, arr.shape[2])  32.5 us
    all_gather x1, waiting for transfers between devices, fetch_fourth(): return lax.all_gather(shard, 'fsdp', axis=1, tiled=True)  20.5 us
    all_gather x1, waiting for transfers between devices, fetch_first(): return lax.all_gather(shard, 'fsdp', axis=1, tiled=True)  18.9 us
  transfers between devices with their start and end apart: 12, of which 6 were waited for; matrix products, arithmetic and copies ran while one was open for 17% of the time, Pallas kernels for 0%

commit v1 on v0

--- a/solution.py
+++ b/solution.py
@@ -6,6 +6,13 @@
 D = 8192
 NB = 64
 HB = 512
+
+
+def trade_parts(shard, name, split, join):
+    size = lax.axis_size(name)
+    tiles = jnp.stack(jnp.split(shard, size, axis=split), axis=0)
+    tiles = lax.all_to_all(tiles, name, split_axis=0, concat_axis=0)
+    return jnp.concatenate(tiles, axis=join)
 
 
 def gelu_value(v):
@@ -94,9 +101,7 @@
     dpre = (dhidden * gelu_slope(pre)).astype(bf16)
     second_grad = jnp.einsum("cpt,cmt->cpm", mixed_in, dpre, preferred_element_type=f32)
     dz = jnp.einsum("cmt,cpm->cpt", dpre, vtwo, preferred_element_type=f32).astype(bf16)
-    dy = join_units(
-        lax.all_to_all(split_units(dz), "tensor", split_axis=1, concat_axis=0, tiled=True)
-    )
+    dy = join_units(trade_parts(split_units(dz), "tensor", 1, 0))
     first_grad = jnp.einsum("tbi,bjt->bij", inputs, dy, preferred_element_type=f32)
     in_grad = jnp.einsum("bjt,bij->tbi", dy, vone, preferred_element_type=f32).astype(bf16)
     in_grad = in_grad.reshape(tok, local_blocks * block_in)

time: 911 us -> 843 us (0.925)
  waiting for transfers between devices: 666 us -> 604 us
  local copies, waits for them, and re-layouts: 85.6 us -> 74.1 us
  matrix products: 109 us -> 120 us
    all_to_all x1, waiting for transfers between devices: 149 us -> 90 us  [local(): lax.all_to_all(split_units(dw), 'tensor', split_axis=1, concat_axis=0, ti...]
    all_to_all x1, waiting for transfers between devices: 153 us -> 122 us  [local(): lax.all_to_all(split_units(down_part), 'tensor', split_axis=1, concat_axi...]
    all_gather x1, waiting for transfers between devices: 0.01 us -> 26.1 us  [fetch_second(): return lax.all_gather(shard, 'fsdp', axis=1, tiled=True)]
    all_to_all x1, waiting for transfers between devices: 171 us -> 148 us  [local(): lax.all_to_all(split_units(first_out), 'tensor', split_axis=1, concat_axi...]
    all_gather x1, waiting for transfers between devices: 0.01 us -> 22.2 us  [fetch_third(): return lax.all_gather(shard, 'fsdp', axis=1, tiled=True)]
    all_to_all x1 -> x0, local copies, waits for them, and re-layouts: 9.15 us -> none  [local(): lax.all_to_all(split_units(dz), 'tensor', split_axis=1, concat_axis=0, ti...]
    reshape x4 -> x3, local copies, waits for them, and re-layouts: 32.5 us -> 24.2 us  [split_units(): return arr.reshape(arr.shape[0], NB, HB // NB, arr.shape[2])]
    unnamed x17 -> x22, local copies, waits for them, and re-layouts: 16.2 us -> 19.6 us
  transfers between devices with their start and end apart: 12 -> 12, of which waited for: 6 -> 8; matrix products, arithmetic and copies ran while one was open for 17% -> 22% of each run, Pallas kernels for 0% -> 0%
where the time goes in v1:
time: 843 us; the launch traced here: 842 us
  waiting for transfers between devices  604 us (72%)
  matrix products  120 us (14%)
  local copies, waits for them, and re-layouts  74.1 us (9%)
  starting transfers between devices  21.6 us (3%)
  between operations  14.2 us (2%)
    all_to_all x1, waiting for transfers between devices, trade_parts(): tiles = lax.all_to_all(tiles, name, split_axis=0, concat_axis=0)  153 us
    all_to_all x1, waiting for transfers between devices, local(): lax.all_to_all(split_units(first_out), 'tensor', split_axis=1, concat_axi...  148 us
    all_to_all x1, waiting for transfers between devices, local(): lax.all_to_all(split_units(down_part), 'tensor', split_axis=1, concat_axi...  122 us
    all_to_all x1, waiting for transfers between devices, local(): lax.all_to_all(split_units(dw), 'tensor', split_axis=1, concat_axis=0, ti...  90 us
    all_gather x1, waiting for transfers between devices, fetch_second(): return lax.all_gather(shard, 'fsdp', axis=1, tiled=True)  26.1 us
    reshape x3, local copies, waits for them, and re-layouts, split_units(): return arr.reshape(arr.shape[0], NB, HB // NB, arr.shape[2])  24.2 us
    all_gather x1, waiting for transfers between devices, fetch_third(): return lax.all_gather(shard, 'fsdp', axis=1, tiled=True)  22.2 us
    all_gather x1, waiting for transfers between devices, fetch_first(): return lax.all_gather(shard, 'fsdp', axis=1, tiled=True)  21.1 us
  transfers between devices with their start and end apart: 12, of which 8 were waited for; matrix products, arithmetic and copies ran while one was open for 22% of the time, Pallas kernels for 0%

profile of v1, /device:TPU:0, one launch (start us, length us, event | category | flops | bytes accessed | tf_op | source)
XLA Modules:
  0.0 842.2 jit_solution(3518289315139058190)
XLA Ops:
  7.9 21.1 %all-gather.5.cloned.1.call-done = bf16[8,128,512]{2,1,0:T(8,128)(2,1)} async-done(((bf16[8,32,512]{2,1,0:T(8,128)(2,1)}), bf16[8,128,512]{2,1,0:T(8,128)(2,1)}) %all-gather.5.cloned.1.call-update) | async-done | bytes 1048592 | tf_op jit(solution)/shard_map/all_gather | solution.py:30
  29.0 7.5 convert_bitcast_fusion.3
  36.6 8.1 copy.55
  44.7 5.6 all-to-all-start
  51.2 19.4 %all-gather.11.cloned.1.call-done = bf16[8,512,128]{1,2,0:T(8,128)(2,1)} async-done(((bf16[8,128,128]{1,2,0:T(8,128)(2,1)}), bf16[8,512,128]{1,2,0:T(8,128)(2,1)}) %all-gather.11.cloned.1.call-update) | async-done | bytes 1048592 | tf_op jit(solution)/shard_map/all_gather | solution.py:42
  70.6 6.8 convert_bitcast_fusion.1
  77.5 8.1 copy.65
  85.5 148.3 %all-to-all-done = bf16[8,64,8,1024]{3,2,0,1:T(8,128)(2,1)} async-done(((bf16[8,64,8,1024]{3,2,0,1:T(8,128)(2,1)}), bf16[8,64,8,1024]{3,2,0,1:T(8,128)(2,1)}, u32[]{:S(2)}, u32[]{:S(2)}) %all-to-all-start) | async-done | bytes 8388640 | tf_op jit(solution)/shard_map/all_to_all | solution.py:70
  233.9 4.9 all-to-all-start.2
  241.1 8.8 %copy.56 = bf16[8,8,8,8,1024]{4,3,0,1,2:T(8,128)(2,1)} copy(bf16[8,8,8,8,1024]{4,3,0,2,1:T(8,128)(2,1)} %bitcast.1) | data formatting | bytes 16777216 | tf_op jit(solution)/shard_map/all_to_all | solution.py:70
  250.0 26.1 %all-gather.7.cloned.1.call-done = bf16[8,512,512]{2,1,0:T(8,128)(2,1)} async-done(((bf16[8,128,512]{2,1,0:T(8,128)(2,1)}), bf16[8,512,512]{2,1,0:T(8,128)(2,1)}) %all-gather.7.cloned.1.call-update) | async-done | bytes 4194320 | tf_op jit(solution)/shard_map/all_gather | solution.py:34
  276.1 14.8 %fusion.7 = (bf16[8,512,1024]{1,2,0:T(8,128)(2,1)}, f32[8,1024,512]{2,1,0:T(8,128)}) fusion(bf16[8,512,1024]{2,1,0:T(8,128)(2,1)} %bitcast.159, bf16[8,512,512]{2,1,0:T(8,128)(2,1)} %all-gather.7.cloned.1.call-done), kind=kOutput, calls=%fused_computation.10 | convolution fusion | flops 4315938816 | bytes 37748736 | tf_op jit(solution)/shard_map/cpt,cpm->cmt/dot_general | solution.py:72
  290.9 22.2 %all-gather.9.cloned.1.call-done = bf16[8,512,512]{1,2,0:T(8,128)(2,1)} async-done(((bf16[8,128,512]{1,2,0:T(8,128)(2,1)}), bf16[8,512,512]{1,2,0:T(8,128)(2,1)}) %all-gather.9.cloned.1.call-update) | async-done | bytes 4194320 | tf_op jit(solution)/shard_map/all_gather | solution.py:38
  313.2 10.2 %convert_bitcast_fusion.2 = bf16[8,64,8,1024]{3,2,1,0:T(8,128)(2,1)} fusion(bf16[8,512,1024]{1,2,0:T(8,128)(2,1)} %get-tuple-element.24, bf16[8,512,512]{1,2,0:T(8,128)(2,1)} %all-gather.9.cloned.1.call-done), kind=kOutput, calls=%fused_computation.19 | convolution fusion | flops 4299161600 | bytes 20971520 | tf_op jit(solution)/shard_map/cmt,cmn->cnt/dot_general | solution.py:74
  323.4 8.1 copy.60
  331.5 90.0 %all-to-all-done.2 = bf16[8,64,8,1024]{3,2,0,1:T(8,128)(2,1)} async-done(((bf16[8,64,8,1024]{3,2,0,1:T(8,128)(2,1)}), bf16[8,64,8,1024]{3,2,0,1:T(8,128)(2,1)}, u32[]{:S(2)}, u32[]{:S(2)}) %all-to-all-start.2) | async-done | bytes 8388640 | tf_op jit(solution)/shard_map/all_to_all | solution.py:91
  421.5 5.0 all-to-all-start.1
  426.8 8.4 copy.66
  435.2 11.0 %convolution_convert_fusion = bf16[8,512,512]{2,1,0:T(8,128)(2,1)} fusion(bf16[8,512,1024]{1,2,0:T(8,128)(2,1)} %get-tuple-element.24, bf16[8,512,1024]{2,1,0:T(8,128)(2,1)} %bitcast.161), kind=kOutput, calls=%fused_computation.23 | convolution fusion | flops 4297064448 | bytes 20971520 | tf_op jit(solution)/shard_map/cmt,cnt->cmn/dot_general | solution.py:99
  446.3 18.1 %fusion.5 = bf16[8,512,1024]{1,2,0:T(8,128)(2,1)} fusion(f32[8,1024,512]{2,1,0:T(8,128)} %get-tuple-element.25, bf16[8,512,1024]{2,1,0:T(8,128)(2,1)} %bitcast.162, bf16[8,512,512]{1,2,0:T(8,128)(2,1)} %all-gather.9.cloned.1.call-done), kind=kOutput, calls=%fused_computation.6 | convolution fusion | flops 4336910336 | bytes 37748736 | tf_op jit(solution)/shard_map/cnt,cmn->cmt/dot_general | solution.py:100
  464.4 12.8 %convert_bitcast_fusion = bf16[8,64,8,1024]{3,2,1,0:T(8,128)(2,1)S(1)} fusion(bf16[8,512,1024]{1,2,0:T(8,128)(2,1)} %fusion.5, bf16[8,512,512]{2,1,0:T(8,128)(2,1)S(1)} %copy-done.4), kind=kOutput, calls=%fused_computation.17 | convolution fusion | flops 4299161600 | bytes 20971520 | tf_op jit(solution)/shard_map/cmt,cpm->cpt/dot_general | solution.py:103
  486.0 122.5 %all-to-all-done.1 = bf16[8,64,8,1024]{3,2,0,1:T(8,128)(2,1)} async-done(((bf16[8,64,8,1024]{3,2,0,1:T(8,128)(2,1)}), bf16[8,64,8,1024]{3,2,0,1:T(8,128)(2,1)}, u32[]{:S(2)}, u32[]{:S(2)}) %all-to-all-start.1) | async-done | bytes 8388640 | tf_op jit(solution)/shard_map/all_to_all | solution.py:77
  608.4 5.0 all-to-all-start.3
  613.5 12.3 %convolution_convert_fusion.1 = bf16[8,512,512]{2,1,0:T(8,128)(2,1)} fusion(bf16[8,512,1024]{2,1,0:T(8,128)(2,1)} %bitcast.160, bf16[8,512,1024]{1,2,0:T(8,128)(2,1)} %fusion.5), kind=kOutput, calls=%fused_computation.24 | convolution fusion | flops 4297064448 | bytes 20971520 | tf_op jit(solution)/shard_map/cpt,cmt->cpm/dot_general | solution.py:102
  626.2 9.1 %copy.61 = bf16[8,8,8,8,1024]{4,3,1,0,2:T(8,128)(2,1)} copy(bf16[8,8,8,8,1024]{4,3,1,2,0:T(8,128)(2,1)} %bitcast.10) | data formatting | bytes 16777216 | tf_op jit(solution)/shard_map/all_to_all | solution.py:77
  635.3 7.1 fusion.28
  642.5 153.2 %all-to-all-done.3 = bf16[8,8,8,8,1024]{4,3,2,1,0:T(8,128)(2,1)} async-done(((bf16[8,8,8,8,1024]{4,3,2,1,0:T(8,128)(2,1)}), bf16[8,8,8,8,1024]{4,3,2,1,0:T(8,128)(2,1)}, u32[]{:S(2)}, u32[]{:S(2)}) %all-to-all-start.3) | async-done | bytes 8388640 | tf_op jit(solution)/shard_map/all_to_all | solution.py:14
  795.6 7.3 fusion.36
  811.5 6.1 convolution_convert_fusion.2
  817.6 3.9 copy.76
  821.5 6.3 fusion.21
  827.8 3.9 copy.77
  (45 shorter events, 25.6 us)
Async XLA Ops:
  7.2 63.5 %copy-start = (bf16[1024,1024]{1,0:T(8,128)(2,1)S(1)}, bf16[1024,1024]{1,0:T(8,128)(2,1)}, u32[]{:S(2)}) copy-start(bf16[1024,1024]{1,0:T(8,128)(2,1)} %param.11) | copy-start | bytes 6291460
  7.2 21.9 %all-gather.5.cloned.1.call-start = ((), (), s32[]{:S(2)}) async-start(), calls=%async_computation.8 | async-start | bytes 1310720 | tf_op jit(solution)/shard_map/all_gather | solution.py:30
  44.7 5.7 copy-start.3
  44.7 189.2 %all-to-all-start = ((bf16[8,64,8,1024]{3,2,0,1:T(8,128)(2,1)}), bf16[8,64,8,1024]{3,2,0,1:T(8,128)(2,1)}, u32[]{:S(2)}, u32[]{:S(2)}) async-start(bf16[8,64,8,1024]{3,2,0,1:T(8,128)(2,1)} %copy.55), calls=%async_computation | async-start | bytes 16777216 | tf_op jit(solution)/shard_map/all_to_all | solution.py:70
  50.3 20.3 %all-gather.11.cloned.1.call-start = ((), (), s32[]{:S(2)}) async-start(), calls=%async_computation.11 | async-start | bytes 1310720 | tf_op jit(solution)/shard_map/all_gather | solution.py:42
  85.5 154.3 %copy-start.2 = (bf16[8,128,512]{2,1,0:T(8,128)(2,1)S(1)}, bf16[8,128,512]{2,1,0:T(8,128)(2,1)}, u32[]{:S(2)}) copy-start(bf16[8,128,512]{2,1,0:T(8,128)(2,1)} %param.9) | copy-start | bytes 3145732
  233.9 187.6 %all-to-all-start.2 = ((bf16[8,64,8,1024]{3,2,0,1:T(8,128)(2,1)}), bf16[8,64,8,1024]{3,2,0,1:T(8,128)(2,1)}, u32[]{:S(2)}, u32[]{:S(2)}) async-start(bf16[8,64,8,1024]{3,2,0,1:T(8,128)(2,1)} %copy.65), calls=%async_computation.2 | async-start | bytes 16777216 | tf_op jit(solution)/shard_map/all_to_all | solution.py:91
  238.8 37.3 %all-gather.7.cloned.1.call-start = ((), (), s32[]{:S(2)}) async-start(), calls=%async_computation.9 | async-start | bytes 5242880 | tf_op jit(solution)/shard_map/all_gather | solution.py:34
  239.6 73.6 %all-gather.9.cloned.1.call-start = ((), (), s32[]{:S(2)}) async-start(), calls=%async_computation.10 | async-start | bytes 5242880 | tf_op jit(solution)/shard_map/all_gather | solution.py:38
  421.5 187.0 %all-to-all-start.1 = ((bf16[8,64,8,1024]{3,2,0,1:T(8,128)(2,1)}), bf16[8,64,8,1024]{3,2,0,1:T(8,128)(2,1)}, u32[]{:S(2)}, u32[]{:S(2)}) async-start(bf16[8,64,8,1024]{3,2,0,1:T(8,128)(2,1)} %copy.60), calls=%async_computation.1 | async-start | bytes 16777216 | tf_op jit(solution)/shard_map/all_to_all | solution.py:77
  426.5 379.2 %reduce-scatter.9.cloned.1.call-start = ((), (), s32[]{:S(2)}) async-start(), calls=%async_computation.14 | async-start | bytes 5242880 | tf_op jit(solution)/shard_map/reduce_scatter | solution.py:115
  446.3 18.2 %copy-start.4 = (bf16[8,512,512]{2,1,0:T(8,128)(2,1)S(1)}, bf16[8,512,512]{2,1,0:T(8,128)(2,1)}, u32[]{:S(2)}) copy-start(bf16[8,512,512]{2,1,0:T(8,128)(2,1)} %all-gather.7.cloned.1.call-done) | copy-start | bytes 12582916
  608.4 187.2 %all-to-all-start.3 = ((bf16[8,8,8,8,1024]{4,3,2,1,0:T(8,128)(2,1)}), bf16[8,8,8,8,1024]{4,3,2,1,0:T(8,128)(2,1)}, u32[]{:S(2)}, u32[]{:S(2)}) async-start(bf16[8,8,8,8,1024]{4,3,2,1,0:T(8,128)(2,1)} %fusion.41), calls=%async_computation.3 | async-start | bytes 16777216 | tf_op jit(solution)/shard_map/all_to_all | solution.py:14
  613.4 195.1 %reduce-scatter.7.cloned.1.call-start = ((), (), s32[]{:S(2)}) async-start(), calls=%async_computation.13 | async-start | bytes 5242880 | tf_op jit(solution)/shard_map/reduce_scatter | solution.py:112
  625.8 205.9 %reduce-scatter.11.cloned.1.call-start = ((), (), s32[]{:S(2)}) async-start(), calls=%async_computation.15 | async-start | bytes 1310720 | tf_op jit(solution)/shard_map/reduce_scatter | solution.py:118
  642.4 191.2 %reduce-scatter.5.cloned.1.call-start = ((), (), s32[]{:S(2)}) async-start(), calls=%async_computation.12 | async-start | bytes 1310720 | tf_op jit(solution)/shard_map/reduce_scatter | solution.py:109
  802.9 8.6 %copy-start.1 = (bf16[8,512,128]{1,2,0:T(8,128)(2,1)S(1)}, bf16[8,512,128]{1,2,0:T(8,128)(2,1)}, u32[]{:S(2)}) copy-start(bf16[8,512,128]{1,2,0:T(8,128)(2,1)} %all-gather.11.cloned.1.call-done) | copy-start | bytes 3145732
Sparse Core Ops, SparseCore 0:
  9.6 19.4 all-gather.4
  53.3 17.3 all-gather.10
  241.2 34.8 all-gather.6
  278.1 35.0 all-gather.8
  446.4 44.6 reduce-scatter.8
  626.0 44.8 reduce-scatter.6
  673.3 24.8 reduce-scatter.10
  805.8 23.2 reduce-scatter.4
